TPU v7x, 512 devices: a whole 4x8x8 slice. The times are simulated.
512 devices in a mesh: ctx: 16 (over z, core), head: 32 (over x, y).
Axes of the slice: x: 4, y: 8, z: 8, core: 2. Of those that a mesh axis runs over, the one named last changes fastest.
Arguments:
- x_in: bfloat16 [4096, 16384], P(('ctx', 'head')), may hold values from -6 to 6
- grad_y: bfloat16 [4096, 16384], P(('ctx', 'head')), may hold values from -6 to 6
- b_in: bfloat16 [4096, 2048], P(('ctx', 'head')), may hold values from -0.29882812 to 0.29882812
- c_in: bfloat16 [4096, 2048], P(('ctx', 'head')), may hold values from -0.375 to 0.375
- dt: bfloat16 [4096, 256], P(('ctx', 'head')), may hold values from 0.25 to 2
- conv_weight: float32 [4, 16384], P(None, 'head'), may hold values from -3 to 3
- conv_bias: float32 [16384], P('head'), may hold values from -3 to 3
- decay_rate: float32 [256], P('head'), may hold values from 1e-05 to 0.02
- skip: float32 [256], P('head'), may hold values from 0.5 to 1.5
Outputs:
- grad_x: bfloat16 [4096, 16384], P(('ctx', 'head'))
- grad_b: bfloat16 [4096, 2048], P(('ctx', 'head'))
- grad_c: bfloat16 [4096, 2048], P(('ctx', 'head'))
- grad_dt: float32 [4096, 256], P(('ctx', 'head'))
All inputs are finite; a program needn't handle non-finite values.
Results may differ from a plain program's by a relative error of at most 0.001.
Values may be sent and summed in bfloat16 or wider, within the bound.
A program may use at most 64 MiB of HBM per device.

v0:
```python
import math
import jax
import jax.numpy as jnp
from jax import lax
from jax.sharding import PartitionSpec as P

HEAD_DIM = 64
STATE = 256
GROUPS = 8
CONV = 4
HIGH = lax.Precision.HIGHEST


def passed_along(value, axis, by):
    count = lax.axis_size(axis)
    pairs = [(i, i + by) for i in range(count) if 0 <= i + by < count]
    return lax.ppermute(value, axis, pairs)


def entering(value, axis, combine, identity, reverse):
    count, place = (lax.axis_size(axis), lax.axis_index(axis))
    everything = jax.tree.map(lambda part: lax.all_gather(part, axis), value)
    start = jax.tree.map(
        lambda part, zero: jnp.broadcast_to(jnp.asarray(zero, part.dtype), part.shape),
        value,
        identity,
    )

    def hop(k, before):
        at = count - 1 - k if reverse else k
        reached = at > place if reverse else at < place
        new = combine(before, jax.tree.map(lambda part: part[at], everything))
        return jax.tree.map(lambda a, b: jnp.where(reached, a, b), new, before)

    return lax.fori_loop(0, count, hop, start)


def conv_silu(padded, weight, bias):
    length = padded.shape[0] - CONV + 1
    summed = bias[None, :] + weight[0][None, :] * padded[0:length]
    for k in range(1, CONV):
        summed = summed + weight[k][None, :] * padded[k : k + length]
    return jax.nn.silu(summed)


def head_forward(
    ext_rows, dt_head, gram_blocks, b_rows, c_rows, weight, bias, head_rate, skip_head, state_in
):
    activ = conv_silu(ext_rows, weight, bias)
    length = activ.shape[0]
    width = gram_blocks.shape[1]
    count = length // width
    causal = lax.broadcasted_iota(jnp.int32, (width, width), 0) >= lax.broadcasted_iota(
        jnp.int32, (width, width), 1
    )
    pieces = (
        activ.reshape(count, width, HEAD_DIM),
        dt_head.reshape(count, width),
        gram_blocks,
        b_rows.reshape(count, width, STATE),
        c_rows.reshape(count, width, STATE),
    )

    def advance(carried, piece):
        act_part, dt_part, gram_part, b_part, c_part = piece
        cumul = jnp.cumsum(-dt_part * head_rate)
        gaps = cumul[:, None] - cumul[None, :]
        decay_mat = jnp.where(causal, jnp.exp(jnp.where(causal, gaps, 0.0)), 0.0)
        mixing = decay_mat * gram_part * dt_part[None, :]
        output = jnp.dot(mixing, act_part, precision=HIGH)
        output = output + jnp.exp(cumul)[:, None] * jnp.dot(c_part, carried.T, precision=HIGH)
        tail_wt = jnp.exp(cumul[-1] - cumul) * dt_part
        carried = jnp.exp(cumul[-1]) * carried + jnp.dot(
            (act_part * tail_wt[:, None]).T, b_part, precision=HIGH
        )
        return (carried, output)

    state_out, outputs = lax.scan(advance, state_in, pieces)
    output = outputs.reshape(length, HEAD_DIM) + skip_head * activ
    return (output, state_out)


def forward_combine(earlier, later):
    return (earlier[0] * later[0], later[0][:, None, None] * earlier[1] + later[1])


def backward_combine(earlier, later):
    return (earlier[0] * later[0], later[1] + later[0][:, None, None] * earlier[1])


def shards(x_in, grad_y, b_in, c_in, dt, conv_weight, conv_bias, decay_rate, skip):
    n_head = lax.axis_size("head")
    per_group = n_head // GROUPS
    tok_dev = x_in.shape[0]
    heads_dev = decay_rate.shape[0]
    x_rows, dy_rows, dt_rows = (
        lax.all_to_all(x_in, "head", split_axis=1, concat_axis=0, tiled=True),
        lax.all_to_all(grad_y, "head", split_axis=1, concat_axis=0, tiled=True),
        lax.all_to_all(dt, "head", split_axis=1, concat_axis=0, tiled=True),
    )
    b_all, c_all = (
        lax.all_gather(b_in, "head", axis=0, tiled=True),
        lax.all_gather(c_in, "head", axis=0, tiled=True),
    )
    first = lax.axis_index("head") // per_group * STATE
    b_rows = lax.dynamic_slice_in_dim(b_all, first, STATE, 1)
    c_rows = lax.dynamic_slice_in_dim(c_all, first, STATE, 1)
    length = x_rows.shape[0]
    width = math.gcd(length, 128)
    count = length // width
    edge = passed_along(x_rows[length - CONV + 1 :], "ctx", 1)
    ext_rows = jnp.concatenate([edge, x_rows], axis=0).astype(jnp.float32)
    b_mat = b_rows.astype(jnp.float32)
    c_mat = c_rows.astype(jnp.float32)
    dt_mat = dt_rows.astype(jnp.float32)
    dy_mat = dy_rows.astype(jnp.float32).reshape(length, heads_dev, HEAD_DIM)
    activ = conv_silu(ext_rows, conv_weight, conv_bias).reshape(length, heads_dev, HEAD_DIM)
    cumul = jnp.cumsum(-dt_mat * decay_rate[None, :], axis=0)
    block_decay = jnp.exp(cumul[-1])
    tail_wt = jnp.exp(cumul[-1][None, :] - cumul) * dt_mat
    local_state = jnp.einsum("shp,sn->hpn", activ * tail_wt[:, :, None], b_mat, precision=HIGH)
    local_pull = jnp.einsum(
        "shp,sn->hpn", dy_mat * jnp.exp(cumul)[:, :, None], c_mat, precision=HIGH
    )
    identity = (
        jnp.ones((heads_dev,), jnp.float32),
        jnp.zeros((heads_dev, HEAD_DIM, STATE), jnp.float32),
    )
    _, state_in = entering((block_decay, local_state), "ctx", forward_combine, identity, False)
    _, state_grad = entering((block_decay, local_pull), "ctx", backward_combine, identity, True)
    b_blocks = b_mat.reshape(count, width, STATE)
    c_blocks = c_mat.reshape(count, width, STATE)
    gram_blocks = jnp.einsum("cwn,cvn->cwv", c_blocks, b_blocks, precision=HIGH)

    def head_step(sums, pieces):
        ext_head, dt_head, weight, bias, head_rate, skip_head, head_state, dy_head, head_grad = (
            pieces
        )

        def forward_fn(ext_arg, dt_arg, gram_arg, b_arg, c_arg):
            return head_forward(
                ext_arg,
                dt_arg,
                gram_arg,
                b_arg,
                c_arg,
                weight,
                bias,
                head_rate,
                skip_head,
                head_state,
            )

        _, pullback = jax.vjp(forward_fn, ext_head, dt_head, gram_blocks, b_mat, c_mat)
        g_ext, g_dt, g_gram, g_b, g_c = pullback((dy_head, head_grad))
        return ((sums[0] + g_gram, sums[1] + g_b, sums[2] + g_c), (g_ext, g_dt))

    ext_heads = ext_rows.reshape(length + CONV - 1, heads_dev, HEAD_DIM).transpose(1, 0, 2)
    weight_heads = conv_weight.reshape(CONV, heads_dev, HEAD_DIM).transpose(1, 0, 2)
    bias_heads = conv_bias.reshape(heads_dev, HEAD_DIM)
    start = (
        jnp.zeros((count, width, width), jnp.float32),
        jnp.zeros((length, STATE), jnp.float32),
        jnp.zeros((length, STATE), jnp.float32),
    )
    inputs = (
        ext_heads,
        dt_mat.T,
        weight_heads,
        bias_heads,
        decay_rate,
        skip,
        state_in,
        dy_mat.transpose(1, 0, 2),
        state_grad,
    )
    sums, per_head = lax.scan(head_step, start, inputs)
    g_gram, g_b, g_c = sums
    g_b = g_b + jnp.einsum("cwv,cwn->cvn", g_gram, c_blocks, precision=HIGH).reshape(length, STATE)
    g_c = g_c + jnp.einsum("cwv,cvn->cwn", g_gram, b_blocks, precision=HIGH).reshape(length, STATE)
    g_ext = per_head[0].transpose(1, 0, 2).reshape(length + CONV - 1, heads_dev * HEAD_DIM)
    g_dt = per_head[1].T
    carried_back = passed_along(g_ext[: CONV - 1], "ctx", -1)
    g_local = g_ext[CONV - 1 :]
    g_local = g_local.at[length - CONV + 1 :].add(carried_back)
    grad_x = lax.all_to_all(
        g_local.astype(jnp.bfloat16), "head", split_axis=0, concat_axis=1, tiled=True
    )
    grad_dt, b_parts, c_parts = (
        lax.all_to_all(g_dt, "head", split_axis=0, concat_axis=1, tiled=True),
        lax.all_to_all(g_b, "head", split_axis=0, concat_axis=1, tiled=True),
        lax.all_to_all(g_c, "head", split_axis=0, concat_axis=1, tiled=True),
    )
    grad_b = (
        b_parts.reshape(tok_dev, GROUPS, per_group, STATE)
        .sum(axis=2)
        .reshape(tok_dev, GROUPS * STATE)
    )
    grad_c = (
        c_parts.reshape(tok_dev, GROUPS, per_group, STATE)
        .sum(axis=2)
        .reshape(tok_dev, GROUPS * STATE)
    )
    return (grad_x, grad_b.astype(jnp.bfloat16), grad_c.astype(jnp.bfloat16), grad_dt)


def solution(mesh):
    in_specs = (
        P(("ctx", "head"), None),
        P(("ctx", "head"), None),
        P(("ctx", "head"), None),
        P(("ctx", "head"), None),
        P(("ctx", "head"), None),
        P(None, "head"),
        P("head"),
        P("head"),
        P("head"),
    )
    out_specs = (
        P(("ctx", "head"), None),
        P(("ctx", "head"), None),
        P(("ctx", "head"), None),
        P(("ctx", "head"), None),
    )
    return jax.shard_map(shards, mesh=mesh, in_specs=in_specs, out_specs=out_specs, check_vma=False)
```

profile of v0, /device:TPU:1, one launch (start us, length us, event | category | flops | bytes accessed | tf_op | source)
XLA Modules:
  0.0 932.1 jit_solution(3826005962519937768)
XLA Ops:
  10.1 10.5 %all-to-all-start.1 = ((bf16[8,32,8]{2,0,1:T(8,128)(2,1)}), bf16[8,32,8]{2,0,1:T(8,128)(2,1)S(1)}, u32[]{:S(2)}, u32[]{:S(2)}) async-start(bf16[8,32,8]{2,0,1:T(8,128)(2,1)} %copy.117), calls=%async_computation.1 | async-start | bytes 131072 | tf_op jit(solution)/shard_map/all_to_all | solution.py:99
  20.7 8.8 all-to-all-done.1
  29.5 3.9 all-to-all-start
  35.9 7.2 all-to-all-done
  45.9 48.0 %all-gather.8.cloned.1.call-done = bf16[256,2048]{1,0:T(8,128)(2,1)} async-done(((bf16[8,2048]{1,0:T(8,128)(2,1)}), bf16[256,2048]{1,0:T(8,128)(2,1)}) %all-gather.8.cloned.1.call-update) | async-done | bytes 1048592 | tf_op jit(solution)/shard_map/all_gather | solution.py:103
  96.7 5.7 all-to-all-start.2
  102.6 9.4 %all-to-all-done.2 = bf16[8,32,512]{2,0,1:T(8,128)(2,1)S(1)} async-done(((bf16[8,32,512]{2,0,1:T(8,128)(2,1)}), bf16[8,32,512]{2,0,1:T(8,128)(2,1)S(1)}, u32[]{:S(2)}, u32[]{:S(2)}) %all-to-all-start.2) | async-done | bytes 262176 | tf_op jit(solution)/shard_map/all_to_all | solution.py:97
  112.0 9.9 %collective-permute-start = (bf16[3,512]{1,0:T(4,128)(2,1)S(1)}, bf16[3,512]{1,0:T(4,128)(2,1)S(1)}, u32[]{:S(2)}, u32[]{:S(2)}) collective-permute-start(bf16[3,512]{1,0:T(4,128)(2,1)S(1)} %slice.212), channel_id=1, source_target_pairs={{0,32},{32,64},{64,96},{96,128},{128,160},{160,192},{192,224},{224... | collective-permute-start | bytes 9224 | tf_op jit(solution)/shard_map/ppermute | solution.py:17
  123.4 53.1 %all-gather.10.cloned.1.call-done = bf16[256,2048]{1,0:T(8,128)(2,1)} async-done(((bf16[8,2048]{1,0:T(8,128)(2,1)}), bf16[256,2048]{1,0:T(8,128)(2,1)}) %all-gather.10.cloned.1.call-update) | async-done | bytes 1048592 | tf_op jit(solution)/shard_map/all_gather | solution.py:102
  180.1 22.8 %all-gather.2 = f32[16,1,8]{2,1,0:T(1,128)S(1)} all-gather(f32[1,1,8]{2,1,0:T(1,128)S(1)} %bitcast.532), channel_id=1, replica_groups=mesh['ctx'=16,'head'=32] {'ctx'}, dimensions={0}, use_global_device_ids=true | all-gather | bytes 544 | tf_op jit(solution)/shard_map/all_gather | solution.py:22
  204.4 36.4 %all-gather.12.cloned.1.call-done = f32[128,64,256]{2,1,0:T(8,128)} async-done(((f32[8,64,256]{2,1,0:T(8,128)}), f32[128,64,256]{2,1,0:T(8,128)}) %all-gather.12.cloned.1.call-update) | async-done | bytes 8388624 | tf_op jit(solution)/shard_map/all_gather | solution.py:22
  240.8 34.0 %while.180 = (s32[]{:T(128)}, f32[8,64,256]{2,1,0:T(8,128)}, s32[]{:T(128)}, f32[16,8,64,256]{3,2,1,0:T(8,128)}, f32[16,8]{1,0:T(8,128)S(1)}, /*index=5*/s32[]{:T(128)}, s32[]{:T(128)}, s32[]{:T(128)}, s32[]{:T(128)}) while((s32[]{:T(128)}, f32[8,64,256]{2,1,0:T(8,128)}, s32[]{:T(128)}, f32[16,8,64,256]{3,2,1,0:T(8,128)}, ...), condition=%wide.region_5.6_spmd.clone, body=%wide.region_4.5_spmd.clone.sunk | while | flops 524296 | bytes 1573127 | solution.py:35
  274.8 25.4 %all-gather.14.cloned.1.call-done = f32[128,64,256]{2,1,0:T(8,128)} async-done(((f32[8,64,256]{2,1,0:T(8,128)}), f32[128,64,256]{2,1,0:T(8,128)}) %all-gather.14.cloned.1.call-update) | async-done | bytes 8388624 | tf_op jit(solution)/shard_map/all_gather | solution.py:22
  300.2 19.4 %while.181 = (s32[]{:T(128)}, f32[8,64,256]{2,1,0:T(8,128)S(1)}, s32[]{:T(128)}, f32[16,8]{1,0:T(8,128)S(1)}, f32[16,8,64,256]{3,2,1,0:T(8,128)}, /*index=5*/s32[]{:T(128)}, s32[]{:T(128)}) while((s32[]{:T(128)}, f32[8,64,256]{2,1,0:T(8,128)S(1)}, s32[]{:T(128)}, f32[16,8]{1,0:T(8,128)S(1)}, f32[16,8,64,256]{3,2,1,0:T(8,128)}, ...), condition=%wide.region_3.4_spmd.clone, body=%wide.region_2.3_spmd.clone.sunk | while | flops 524292 | bytes 1573065 | solution.py:35
  319.6 532.5 %while.184 = (s32[]{:T(128)}, f32[2,128,128]{2,1,0:T(8,128)}, f32[256,256]{1,0:T(8,128)}, f32[256,256]{1,0:T(8,128)}, f32[8,259,64]{1,2,0:T(8,128)}, /*index=5*/...) while((s32[]{:T(128)}, f32[2,128,128]{2,1,0:T(8,128)}, ...), condition=%wide.region_20.21_spmd.clone, body=%wide.region_6.20_spmd.clone.sunk | while | flops 177621440 | bytes 10403926 | solution.py:177
  320.4 2.9 constant_dynamic-slice_fusion.26
  327.2 12.2 %while.185 = (s32[]{:T(128)}, f32[64,256]{1,0:T(8,128)S(1)}, f32[2,128,128]{2,1,0:T(8,128)S(1)}, f32[2,128,128]{2,1,0:T(8,128)S(1)}, f32[2,1,128]{2,1,0:T(1,128)...) while((s32[]{:T(128)}, f32[64,256]{1,0:T(8,128)S(1)}, ...), condition=%wide.region_9.9_spmd.clone.clone, body=%wide.region_7.8_spmd.clone.clone.sunk | while | flops 50496128 | bytes 1198381 | solution.py:78
  343.5 32.7 %while.186 = (s32[]{:T(128)}, f32[64,256]{1,0:T(8,128)S(1)}, f32[2,128,64]{1,2,0:T(8,128)}, f32[2,128]{1,0:T(2,128)}, f32[2,128,128]{2,1,0:T(8,128)}, /*index=5*...) while((s32[]{:T(128)}, f32[64,256]{1,0:T(8,128)S(1)}, ...), condition=%wide.region_19.19_spmd.clone.clone, body=%wide.region_10.18_spmd.clone.clone.sunk | while | flops 126174464 | bytes 2319733 | solution.py:78
  386.0 2.9 constant_dynamic-slice_fusion.26
  392.8 12.2 %while.185 = (s32[]{:T(128)}, f32[64,256]{1,0:T(8,128)S(1)}, f32[2,128,128]{2,1,0:T(8,128)S(1)}, f32[2,128,128]{2,1,0:T(8,128)S(1)}, f32[2,1,128]{2,1,0:T(1,128)...) while((s32[]{:T(128)}, f32[64,256]{1,0:T(8,128)S(1)}, ...), condition=%wide.region_9.9_spmd.clone.clone, body=%wide.region_7.8_spmd.clone.clone.sunk | while | flops 50496128 | bytes 1198381 | solution.py:78
  409.1 32.7 %while.186 = (s32[]{:T(128)}, f32[64,256]{1,0:T(8,128)S(1)}, f32[2,128,64]{1,2,0:T(8,128)}, f32[2,128]{1,0:T(2,128)}, f32[2,128,128]{2,1,0:T(8,128)}, /*index=5*...) while((s32[]{:T(128)}, f32[64,256]{1,0:T(8,128)S(1)}, ...), condition=%wide.region_19.19_spmd.clone.clone, body=%wide.region_10.18_spmd.clone.clone.sunk | while | flops 126174464 | bytes 2319733 | solution.py:78
  452.7 2.9 constant_dynamic-slice_fusion.26
  459.5 12.2 %while.185 = (s32[]{:T(128)}, f32[64,256]{1,0:T(8,128)S(1)}, f32[2,128,128]{2,1,0:T(8,128)S(1)}, f32[2,128,128]{2,1,0:T(8,128)S(1)}, f32[2,1,128]{2,1,0:T(1,128)...) while((s32[]{:T(128)}, f32[64,256]{1,0:T(8,128)S(1)}, ...), condition=%wide.region_9.9_spmd.clone.clone, body=%wide.region_7.8_spmd.clone.clone.sunk | while | flops 50496128 | bytes 1198381 | solution.py:78
  475.8 32.7 %while.186 = (s32[]{:T(128)}, f32[64,256]{1,0:T(8,128)S(1)}, f32[2,128,64]{1,2,0:T(8,128)}, f32[2,128]{1,0:T(2,128)}, f32[2,128,128]{2,1,0:T(8,128)}, /*index=5*...) while((s32[]{:T(128)}, f32[64,256]{1,0:T(8,128)S(1)}, ...), condition=%wide.region_19.19_spmd.clone.clone, body=%wide.region_10.18_spmd.clone.clone.sunk | while | flops 126174464 | bytes 2319733 | solution.py:78
  519.4 2.9 constant_dynamic-slice_fusion.26
  526.2 12.2 %while.185 = (s32[]{:T(128)}, f32[64,256]{1,0:T(8,128)S(1)}, f32[2,128,128]{2,1,0:T(8,128)S(1)}, f32[2,128,128]{2,1,0:T(8,128)S(1)}, f32[2,1,128]{2,1,0:T(1,128)...) while((s32[]{:T(128)}, f32[64,256]{1,0:T(8,128)S(1)}, ...), condition=%wide.region_9.9_spmd.clone.clone, body=%wide.region_7.8_spmd.clone.clone.sunk | while | flops 50496128 | bytes 1198381 | solution.py:78
  542.5 32.7 %while.186 = (s32[]{:T(128)}, f32[64,256]{1,0:T(8,128)S(1)}, f32[2,128,64]{1,2,0:T(8,128)}, f32[2,128]{1,0:T(2,128)}, f32[2,128,128]{2,1,0:T(8,128)}, /*index=5*...) while((s32[]{:T(128)}, f32[64,256]{1,0:T(8,128)S(1)}, ...), condition=%wide.region_19.19_spmd.clone.clone, body=%wide.region_10.18_spmd.clone.clone.sunk | while | flops 126174464 | bytes 2319733 | solution.py:78
  586.1 2.9 constant_dynamic-slice_fusion.26
  592.9 12.2 %while.185 = (s32[]{:T(128)}, f32[64,256]{1,0:T(8,128)S(1)}, f32[2,128,128]{2,1,0:T(8,128)S(1)}, f32[2,128,128]{2,1,0:T(8,128)S(1)}, f32[2,1,128]{2,1,0:T(1,128)...) while((s32[]{:T(128)}, f32[64,256]{1,0:T(8,128)S(1)}, ...), condition=%wide.region_9.9_spmd.clone.clone, body=%wide.region_7.8_spmd.clone.clone.sunk | while | flops 50496128 | bytes 1198381 | solution.py:78
  609.2 32.7 %while.186 = (s32[]{:T(128)}, f32[64,256]{1,0:T(8,128)S(1)}, f32[2,128,64]{1,2,0:T(8,128)}, f32[2,128]{1,0:T(2,128)}, f32[2,128,128]{2,1,0:T(8,128)}, /*index=5*...) while((s32[]{:T(128)}, f32[64,256]{1,0:T(8,128)S(1)}, ...), condition=%wide.region_19.19_spmd.clone.clone, body=%wide.region_10.18_spmd.clone.clone.sunk | while | flops 126174464 | bytes 2319733 | solution.py:78
  652.8 2.9 constant_dynamic-slice_fusion.26
  659.5 12.2 %while.185 = (s32[]{:T(128)}, f32[64,256]{1,0:T(8,128)S(1)}, f32[2,128,128]{2,1,0:T(8,128)S(1)}, f32[2,128,128]{2,1,0:T(8,128)S(1)}, f32[2,1,128]{2,1,0:T(1,128)...) while((s32[]{:T(128)}, f32[64,256]{1,0:T(8,128)S(1)}, ...), condition=%wide.region_9.9_spmd.clone.clone, body=%wide.region_7.8_spmd.clone.clone.sunk | while | flops 50496128 | bytes 1198381 | solution.py:78
  675.9 32.7 %while.186 = (s32[]{:T(128)}, f32[64,256]{1,0:T(8,128)S(1)}, f32[2,128,64]{1,2,0:T(8,128)}, f32[2,128]{1,0:T(2,128)}, f32[2,128,128]{2,1,0:T(8,128)}, /*index=5*...) while((s32[]{:T(128)}, f32[64,256]{1,0:T(8,128)S(1)}, ...), condition=%wide.region_19.19_spmd.clone.clone, body=%wide.region_10.18_spmd.clone.clone.sunk | while | flops 126174464 | bytes 2319733 | solution.py:78
  719.5 2.9 constant_dynamic-slice_fusion.26
  726.2 12.2 %while.185 = (s32[]{:T(128)}, f32[64,256]{1,0:T(8,128)S(1)}, f32[2,128,128]{2,1,0:T(8,128)S(1)}, f32[2,128,128]{2,1,0:T(8,128)S(1)}, f32[2,1,128]{2,1,0:T(1,128)...) while((s32[]{:T(128)}, f32[64,256]{1,0:T(8,128)S(1)}, ...), condition=%wide.region_9.9_spmd.clone.clone, body=%wide.region_7.8_spmd.clone.clone.sunk | while | flops 50496128 | bytes 1198381 | solution.py:78
  742.6 32.7 %while.186 = (s32[]{:T(128)}, f32[64,256]{1,0:T(8,128)S(1)}, f32[2,128,64]{1,2,0:T(8,128)}, f32[2,128]{1,0:T(2,128)}, f32[2,128,128]{2,1,0:T(8,128)}, /*index=5*...) while((s32[]{:T(128)}, f32[64,256]{1,0:T(8,128)S(1)}, ...), condition=%wide.region_19.19_spmd.clone.clone, body=%wide.region_10.18_spmd.clone.clone.sunk | while | flops 126174464 | bytes 2319733 | solution.py:78
  786.1 2.9 constant_dynamic-slice_fusion.26
  792.9 12.2 %while.185 = (s32[]{:T(128)}, f32[64,256]{1,0:T(8,128)S(1)}, f32[2,128,128]{2,1,0:T(8,128)S(1)}, f32[2,128,128]{2,1,0:T(8,128)S(1)}, f32[2,1,128]{2,1,0:T(1,128)...) while((s32[]{:T(128)}, f32[64,256]{1,0:T(8,128)S(1)}, ...), condition=%wide.region_9.9_spmd.clone.clone, body=%wide.region_7.8_spmd.clone.clone.sunk | while | flops 50496128 | bytes 1198381 | solution.py:78
  809.3 32.7 %while.186 = (s32[]{:T(128)}, f32[64,256]{1,0:T(8,128)S(1)}, f32[2,128,64]{1,2,0:T(8,128)}, f32[2,128]{1,0:T(2,128)}, f32[2,128,128]{2,1,0:T(8,128)}, /*index=5*...) while((s32[]{:T(128)}, f32[64,256]{1,0:T(8,128)S(1)}, ...), condition=%wide.region_19.19_spmd.clone.clone, body=%wide.region_10.18_spmd.clone.clone.sunk | while | flops 126174464 | bytes 2319733 | solution.py:78
  854.8 9.3 all-to-all-start.6
  865.8 7.5 all-to-all-done.6
  873.2 4.6 all-to-all-start.5
  880.8 6.7 all-to-all-done.5
  887.5 6.3 all-to-all-start.4
  894.8 3.8 collective-permute-start.1
  899.9 2.9 collective-permute-done.1
  904.5 8.9 all-to-all-start.3
  915.4 9.4 %all-to-all-done.3 = bf16[32,8,512]{2,1,0:T(8,128)(2,1)S(1)} async-done(((bf16[32,8,512]{2,1,0:T(8,128)(2,1)}), bf16[32,8,512]{2,1,0:T(8,128)(2,1)S(1)}, u32[]{:S(2)}, u32[]{:S(2)}) %all-to-all-start.3) | async-done | bytes 262176 | tf_op jit(solution)/shard_map/all_to_all | solution.py:186
  (1223 shorter events, 561.3 us)
Async XLA Ops:
  7.2 95.2 %copy-start.11 = (f32[4,512]{1,0:T(4,128)S(1)}, f32[4,512]{1,0:T(4,128)}, u32[]{:S(2)}) copy-start(f32[4,512]{1,0:T(4,128)} %param.26) | copy-start | bytes 24580
  7.2 115.6 %copy-start.12 = (f32[512]{0:T(512)S(1)}, f32[512]{0:T(512)}, u32[]{:S(2)}) copy-start(f32[512]{0:T(512)} %param.27) | copy-start | bytes 6148
  7.2 86.7 %all-gather.8.cloned.1.call-start = ((), (), s32[]{:S(2)}) async-start(), calls=%async_computation.7 | async-start | bytes 1081344 | tf_op jit(solution)/shard_map/all_gather | solution.py:103
  7.9 168.6 %all-gather.10.cloned.1.call-start = ((), (), s32[]{:S(2)}) async-start(), calls=%async_computation.8 | async-start | bytes 1081344 | tf_op jit(solution)/shard_map/all_gather | solution.py:102
  10.1 19.4 %all-to-all-start.1 = ((bf16[8,32,8]{2,0,1:T(8,128)(2,1)}), bf16[8,32,8]{2,0,1:T(8,128)(2,1)S(1)}, u32[]{:S(2)}, u32[]{:S(2)}) async-start(bf16[8,32,8]{2,0,1:T(8,128)(2,1)} %copy.117), calls=%async_computation.1 | async-start | bytes 131072 | tf_op jit(solution)/shard_map/all_to_all | solution.py:99
  29.5 13.5 %all-to-all-start = ((bf16[8,32,512]{2,0,1:T(8,128)(2,1)}), bf16[8,32,512]{2,0,1:T(8,128)(2,1)S(1)}, u32[]{:S(2)}, u32[]{:S(2)}) async-start(bf16[8,32,512]{2,0,1:T(8,128)(2,1)} %bitcast.520), calls=%async_computation | async-start | bytes 524288 | tf_op jit(solution)/shard_map/all_to_all | solution.py:98
  33.4 207.4 %all-gather.12.cloned.1.call-start = ((), (), s32[]{:S(2)}) async-start(), calls=%async_computation.9 | async-start | bytes 8912896 | tf_op jit(solution)/shard_map/all_gather | solution.py:22
  94.8 146.0 %copy-start.2 = (bf16[256,256]{1,0:T(8,128)(2,1)}, bf16[256,256]{1,0:T(8,128)(2,1)S(1)}, u32[]{:S(2)}) copy-start(bf16[256,256]{1,0:T(8,128)(2,1)S(1)} %get-tuple-element.2368) | copy-start | bytes 393220
  96.7 15.4 %all-to-all-start.2 = ((bf16[8,32,512]{2,0,1:T(8,128)(2,1)}), bf16[8,32,512]{2,0,1:T(8,128)(2,1)S(1)}, u32[]{:S(2)}, u32[]{:S(2)}) async-start(bf16[8,32,512]{2,0,1:T(8,128)(2,1)} %bitcast.16), calls=%async_computation.2 | async-start | bytes 524288 | tf_op jit(solution)/shard_map/all_to_all | solution.py:97
  102.4 197.9 %all-gather.14.cloned.1.call-start = ((), (), s32[]{:S(2)}) async-start(), calls=%async_computation.10 | async-start | bytes 8912896 | tf_op jit(solution)/shard_map/all_gather | solution.py:22
  112.0 10.7 %collective-permute-start = (bf16[3,512]{1,0:T(4,128)(2,1)S(1)}, bf16[3,512]{1,0:T(4,128)(2,1)S(1)}, u32[]{:S(2)}, u32[]{:S(2)}) collective-permute-start(bf16[3,512]{1,0:T(4,128)(2,1)S(1)} %slice.212), channel_id=1, source_target_pairs={{0,32},{32,64},{64,96},{96,128},{128,160},{160,192},{192,224},{224... | collective-permute-start | bytes 9224 | tf_op jit(solution)/shard_map/ppermute | solution.py:17
  177.4 122.8 %copy-start.1 = (bf16[256,256]{1,0:T(8,128)(2,1)}, bf16[256,256]{1,0:T(8,128)(2,1)S(1)}, u32[]{:S(2)}) copy-start(bf16[256,256]{1,0:T(8,128)(2,1)S(1)} %get-tuple-element.2370) | copy-start | bytes 393220
  320.4 6.2 copy-start.3
  320.4 6.2 copy-start.4
  320.4 6.2 copy-start.5
  320.4 6.2 copy-start.9
  386.0 6.2 copy-start.3
  386.0 6.2 copy-start.4
  386.0 6.2 copy-start.5
  386.0 6.2 copy-start.9
  452.7 6.2 copy-start.3
  452.7 6.2 copy-start.4
  452.7 6.2 copy-start.5
  452.7 6.2 copy-start.9
  519.4 6.2 copy-start.3
  519.4 6.2 copy-start.4
  519.4 6.2 copy-start.5
  519.4 6.2 copy-start.9
  586.0 6.2 copy-start.3
  586.0 6.2 copy-start.4
  586.0 6.2 copy-start.5
  586.1 6.2 copy-start.9
  652.7 6.2 copy-start.3
  652.7 6.2 copy-start.4
  652.7 6.2 copy-start.5
  652.8 6.2 copy-start.9
  719.4 6.2 copy-start.3
  719.4 6.2 copy-start.4
  719.4 6.2 copy-start.5
  719.5 6.2 copy-start.9
  786.1 6.2 copy-start.4
  786.1 6.2 copy-start.5
  786.1 6.2 copy-start.9
  854.8 18.4 %all-to-all-start.6 = ((f32[32,8,8]{1,2,0:T(8,128)}), f32[32,8,8]{1,2,0:T(8,128)S(1)}, u32[]{:S(2)}, u32[]{:S(2)}) async-start(f32[32,8,8]{1,2,0:T(8,128)} %copy.135), calls=%async_computation.6 | async-start | bytes 262144 | tf_op jit(solution)/shard_map/all_to_all | solution.py:190
  873.2 14.3 %all-to-all-start.5 = ((f32[32,8,256]{2,1,0:T(8,128)}), f32[32,8,256]{2,1,0:T(8,128)S(1)}, u32[]{:S(2)}, u32[]{:S(2)}) async-start(f32[32,8,256]{2,1,0:T(8,128)} %bitcast.44), calls=%async_computation.5 | async-start | bytes 524288 | tf_op jit(solution)/shard_map/all_to_all | solution.py:192
  887.5 17.0 %all-to-all-start.4 = ((f32[32,8,256]{2,1,0:T(8,128)}), f32[32,8,256]{2,1,0:T(8,128)S(1)}, u32[]{:S(2)}, u32[]{:S(2)}) async-start(f32[32,8,256]{2,1,0:T(8,128)} %bitcast.39), calls=%async_computation.4 | async-start | bytes 524288 | tf_op jit(solution)/shard_map/all_to_all | solution.py:191
  894.8 8.0 collective-permute-start.1
  904.5 20.3 %all-to-all-start.3 = ((bf16[32,8,512]{2,1,0:T(8,128)(2,1)}), bf16[32,8,512]{2,1,0:T(8,128)(2,1)S(1)}, u32[]{:S(2)}, u32[]{:S(2)}) async-start(bf16[32,8,512]{2,1,0:T(8,128)(2,1)} %bitcast.35), calls=%async_computation.3 | async-start | bytes 524288 | tf_op jit(solution)/shard_map/all_to_all | solution.py:186
  (49 other events, 112.6 us)
Sparse Core Ops, SparseCore 0:
  11.2 82.6 all-gather.7
  97.1 79.3 all-gather.9
  178.6 62.1 all-gather.11
  242.8 57.3 all-gather.13
where the time goes:
time: 941 us; the launch traced here: 932 us
  other arithmetic  270 us (29%)
  local copies, waits for them, and re-layouts  240 us (26%)
  waiting for transfers between devices  216 us (23%)
  matrix products  72.4 us (8%)
  starting transfers between devices  63 us (7%)
  loops' own time  33.3 us (4%)
  blocking collectives  22.8 us (2%)
  between operations  14.1 us (1%)
    all_gather x2, waiting for transfers between devices, entering(): everything = jax.tree.map(lambda part: lax.all_gather(part, axis), value)  61.8 us
    all_gather x1, waiting for transfers between devices, shards(): lax.all_gather(b_in, 'head', axis=0, tiled=True)  53.1 us
    select_n x32, other arithmetic, hop(): return jax.tree.map(lambda a, b: jnp.where(reached, a, b), new, before)  52.6 us
    dynamic_update_slice x112, local copies, waits for them, and re-layouts, head_forward(): state_out, outputs = lax.scan(advance, state_in, pieces)  48.8 us
    all_gather x1, waiting for transfers between devices, shards(): lax.all_gather(c_in, 'head', axis=0, tiled=True)  48 us
    another operation x91, other arithmetic  43.5 us
    dynamic_slice x40, local copies, waits for them, and re-layouts, shards(): sums, per_head = lax.scan(head_step, start, inputs)  43.1 us
    another operation x16, loops' own time, head_forward(): state_out, outputs = lax.scan(advance, state_in, pieces)  30.4 us
  transfers between devices with their start and end apart: 13, of which 11 were waited for; matrix products, arithmetic and copies ran while one was open for 6% of the time, Pallas kernels for 0%

commit v1 on v0

--- a/solution.py
+++ b/solution.py
@@ -100,7 +100,9 @@
     )
     b_all, c_all = (
         lax.all_gather(b_in, "head", axis=0, tiled=True),
-        lax.all_gather(c_in, "head", axis=0, tiled=True),
+        jnp.concatenate(
+            lax.all_to_all(jnp.stack([c_in] * lax.axis_size("head")), "head", 0, 0), axis=0
+        ),
     )
     first = lax.axis_index("head") // per_group * STATE
     b_rows = lax.dynamic_slice_in_dim(b_all, first, STATE, 1)

time: 941 us -> 910 us (0.967)
  waiting for transfers between devices: 216 us -> 150 us
  blocking collectives: 22.8 us -> 55.5 us
    all_gather x1 -> x0, waiting for transfers between devices: 48 us -> none  [shards(): lax.all_gather(c_in, 'head', axis=0, tiled=True)]
    all_to_all x0 -> x2, blocking collectives: none -> 32.7 us  [the longest x1 19.2 us: shards(): lax.all_to_all(dt, 'head', split_axis=1, concat_axis=0, tiled=True)]
    all_gather x1, waiting for transfers between devices: 53.1 us -> 35.1 us  [shards(): lax.all_gather(b_in, 'head', axis=0, tiled=True)]
  transfers between devices with their start and end apart: 13 -> 11, of which waited for: 11 -> 9; matrix products, arithmetic and copies ran while one was open for 6% -> 6% of each run, Pallas kernels for 0% -> 0%
where the time goes in v1:
time: 910 us; the launch traced here: 901 us
  other arithmetic  272 us (30%)
  local copies, waits for them, and re-layouts  242 us (27%)
  waiting for transfers between devices  150 us (16%)
  matrix products  74.7 us (8%)
  blocking collectives  55.5 us (6%)
  starting transfers between devices  54.9 us (6%)
  loops' own time  36.3 us (4%)
  between operations  14.1 us (2%)
    all_gather x2, waiting for transfers between devices, entering(): everything = jax.tree.map(lambda part: lax.all_gather(part, axis), value)  61.8 us
    select_n x32, other arithmetic, hop(): return jax.tree.map(lambda a, b: jnp.where(reached, a, b), new, before)  52.8 us
    dynamic_update_slice x112, local copies, waits for them, and re-layouts, head_forward(): state_out, outputs = lax.scan(advance, state_in, pieces)  48.3 us
    another operation x91, other arithmetic  44 us
    dynamic_slice x40, local copies, waits for them, and re-layouts, shards(): sums, per_head = lax.scan(head_step, start, inputs)  43 us
    all_gather x1, waiting for transfers between devices, shards(): lax.all_gather(b_in, 'head', axis=0, tiled=True)  35.1 us
    another operation x16, loops' own time, head_forward(): state_out, outputs = lax.scan(advance, state_in, pieces)  33.4 us
    reduce_sum x16, other arithmetic, advance(): tail_wt = jnp.exp(cumul[-1] - cumul) * dt_part  30 us
  transfers between devices with their start and end apart: 11, of which 9 were waited for; matrix products, arithmetic and copies ran while one was open for 6% of the time, Pallas kernels for 0%

profile of v1, /device:TPU:1, one launch (start us, length us, event | category | flops | bytes accessed | tf_op | source)
XLA Modules:
  0.0 900.5 jit_solution(5044417318300034900)
XLA Ops:
  8.0 19.2 %all_to_all.120 = bf16[8,32,8]{2,0,1:T(8,128)(2,1)S(1)} all-to-all(bf16[8,32,8]{2,0,1:T(8,128)(2,1)S(1)} %copy.117), channel_id=1, replica_groups=mesh['ctx'=16,'head'=32] {'head'}, dimensions={1} | all-to-all | bytes 8192 | tf_op jit(solution)/shard_map/all_to_all | solution.py:99
  27.2 13.5 %all_to_all.121 = bf16[8,32,512]{2,0,1:T(8,128)(2,1)S(1)} all-to-all(bf16[8,32,512]{2,0,1:T(8,128)(2,1)} %bitcast.522), channel_id=1, replica_groups=mesh['ctx'=16,'head'=32] {'head'}, dimensions={1} | all-to-all | bytes 524288 | tf_op jit(solution)/shard_map/all_to_all | solution.py:98
  42.6 5.1 all-to-all-start.2
  53.8 16.6 %all-to-all-done.2 = bf16[32,8,2048]{2,1,0:T(8,128)(2,1)S(1)} async-done(((bf16[32,8,2048]{2,1,0:T(8,128)(2,1)}), bf16[32,8,2048]{2,1,0:T(8,128)(2,1)S(1)}, u32[]{:S(2)}, u32[]{:S(2)}) %all-to-all-start.2) | async-done | bytes 1048608 | tf_op jit(solution)/shard_map/all_to_all | solution.py:104
  72.3 8.0 all-to-all-start.3
  80.6 9.4 %all-to-all-done.3 = bf16[8,32,512]{2,0,1:T(8,128)(2,1)S(1)} async-done(((bf16[8,32,512]{2,0,1:T(8,128)(2,1)}), bf16[8,32,512]{2,0,1:T(8,128)(2,1)S(1)}, u32[]{:S(2)}, u32[]{:S(2)}) %all-to-all-start.3) | async-done | bytes 262176 | tf_op jit(solution)/shard_map/all_to_all | solution.py:97
  89.9 9.1 %collective-permute-start = (bf16[3,512]{1,0:T(4,128)(2,1)S(1)}, bf16[3,512]{1,0:T(4,128)(2,1)S(1)}, u32[]{:S(2)}, u32[]{:S(2)}) collective-permute-start(bf16[3,512]{1,0:T(4,128)(2,1)S(1)} %slice.212), channel_id=1, source_target_pairs={{0,32},{32,64},{64,96},{96,128},{128,160},{160,192},{192,224},{224... | collective-permute-start | bytes 9224 | tf_op jit(solution)/shard_map/ppermute | solution.py:17
  100.5 35.1 %all-gather.7.cloned.1.call-done = bf16[256,2048]{1,0:T(8,128)(2,1)} async-done(((bf16[8,2048]{1,0:T(8,128)(2,1)}), bf16[256,2048]{1,0:T(8,128)(2,1)}) %all-gather.7.cloned.1.call-update) | async-done | bytes 1048592 | tf_op jit(solution)/shard_map/all_gather | solution.py:102
  139.2 22.8 %all-gather.2 = f32[16,1,8]{2,1,0:T(1,128)S(1)} all-gather(f32[1,1,8]{2,1,0:T(1,128)S(1)} %bitcast.535), channel_id=1, replica_groups=mesh['ctx'=16,'head'=32] {'ctx'}, dimensions={0}, use_global_device_ids=true | all-gather | bytes 544 | tf_op jit(solution)/shard_map/all_gather | solution.py:22
  163.6 36.4 %all-gather.9.cloned.1.call-done = f32[128,64,256]{2,1,0:T(8,128)} async-done(((f32[8,64,256]{2,1,0:T(8,128)}), f32[128,64,256]{2,1,0:T(8,128)}) %all-gather.9.cloned.1.call-update) | async-done | bytes 8388624 | tf_op jit(solution)/shard_map/all_gather | solution.py:22
  199.9 34.1 %while.180 = (s32[]{:T(128)}, f32[8,64,256]{2,1,0:T(8,128)}, s32[]{:T(128)}, f32[16,8,64,256]{3,2,1,0:T(8,128)}, f32[16,8]{1,0:T(8,128)S(1)}, /*index=5*/s32[]{:T(128)}, s32[]{:T(128)}, s32[]{:T(128)}, s32[]{:T(128)}) while((s32[]{:T(128)}, f32[8,64,256]{2,1,0:T(8,128)}, s32[]{:T(128)}, f32[16,8,64,256]{3,2,1,0:T(8,128)}, ...), condition=%wide.region_5.6_spmd.clone, body=%wide.region_4.5_spmd.clone.sunk | while | flops 524296 | bytes 1573127 | solution.py:35
  225.4 2.2 fusion.141
  234.1 25.4 %all-gather.11.cloned.1.call-done = f32[128,64,256]{2,1,0:T(8,128)} async-done(((f32[8,64,256]{2,1,0:T(8,128)}), f32[128,64,256]{2,1,0:T(8,128)}) %all-gather.11.cloned.1.call-update) | async-done | bytes 8388624 | tf_op jit(solution)/shard_map/all_gather | solution.py:22
  259.5 19.4 %while.181 = (s32[]{:T(128)}, f32[8,64,256]{2,1,0:T(8,128)S(1)}, s32[]{:T(128)}, f32[16,8]{1,0:T(8,128)S(1)}, f32[16,8,64,256]{3,2,1,0:T(8,128)}, /*index=5*/s32[]{:T(128)}, s32[]{:T(128)}) while((s32[]{:T(128)}, f32[8,64,256]{2,1,0:T(8,128)S(1)}, s32[]{:T(128)}, f32[16,8]{1,0:T(8,128)S(1)}, f32[16,8,64,256]{3,2,1,0:T(8,128)}, ...), condition=%wide.region_3.4_spmd.clone, body=%wide.region_2.3_spmd.clone.sunk | while | flops 524292 | bytes 1573065 | solution.py:35
  278.9 541.8 %while.184 = (s32[]{:T(128)}, f32[2,128,128]{2,1,0:T(8,128)}, f32[256,256]{1,0:T(8,128)}, f32[256,256]{1,0:T(8,128)}, f32[8,259,64]{1,2,0:T(8,128)}, /*index=5*/...) while((s32[]{:T(128)}, f32[2,128,128]{2,1,0:T(8,128)}, ...), condition=%wide.region_20.21_spmd.clone, body=%wide.region_6.20_spmd.clone.sunk | while | flops 177621440 | bytes 10403926 | solution.py:179
  279.6 3.0 constant_dynamic-slice_fusion.26
  286.6 12.2 %while.185 = (s32[]{:T(128)}, f32[64,256]{1,0:T(8,128)S(1)}, f32[2,128,128]{2,1,0:T(8,128)S(1)}, f32[2,128,128]{2,1,0:T(8,128)S(1)}, f32[2,1,128]{2,1,0:T(1,128)...) while((s32[]{:T(128)}, f32[64,256]{1,0:T(8,128)S(1)}, ...), condition=%wide.region_9.9_spmd.clone.clone, body=%wide.region_7.8_spmd.clone.clone.sunk | while | flops 50496128 | bytes 1198381 | solution.py:78
  303.0 33.7 %while.186 = (s32[]{:T(128)}, f32[64,256]{1,0:T(8,128)S(1)}, f32[2,128,64]{1,2,0:T(8,128)}, f32[2,128]{1,0:T(2,128)}, f32[2,128,128]{2,1,0:T(8,128)}, /*index=5*...) while((s32[]{:T(128)}, f32[64,256]{1,0:T(8,128)S(1)}, ...), condition=%wide.region_19.19_spmd.clone.clone, body=%wide.region_10.18_spmd.clone.clone.sunk | while | flops 126174464 | bytes 2319733 | solution.py:78
  346.4 3.0 constant_dynamic-slice_fusion.26
  353.4 12.2 %while.185 = (s32[]{:T(128)}, f32[64,256]{1,0:T(8,128)S(1)}, f32[2,128,128]{2,1,0:T(8,128)S(1)}, f32[2,128,128]{2,1,0:T(8,128)S(1)}, f32[2,1,128]{2,1,0:T(1,128)...) while((s32[]{:T(128)}, f32[64,256]{1,0:T(8,128)S(1)}, ...), condition=%wide.region_9.9_spmd.clone.clone, body=%wide.region_7.8_spmd.clone.clone.sunk | while | flops 50496128 | bytes 1198381 | solution.py:78
  369.8 33.7 %while.186 = (s32[]{:T(128)}, f32[64,256]{1,0:T(8,128)S(1)}, f32[2,128,64]{1,2,0:T(8,128)}, f32[2,128]{1,0:T(2,128)}, f32[2,128,128]{2,1,0:T(8,128)}, /*index=5*...) while((s32[]{:T(128)}, f32[64,256]{1,0:T(8,128)S(1)}, ...), condition=%wide.region_19.19_spmd.clone.clone, body=%wide.region_10.18_spmd.clone.clone.sunk | while | flops 126174464 | bytes 2319733 | solution.py:78
  414.3 3.0 constant_dynamic-slice_fusion.26
  421.3 12.2 %while.185 = (s32[]{:T(128)}, f32[64,256]{1,0:T(8,128)S(1)}, f32[2,128,128]{2,1,0:T(8,128)S(1)}, f32[2,128,128]{2,1,0:T(8,128)S(1)}, f32[2,1,128]{2,1,0:T(1,128)...) while((s32[]{:T(128)}, f32[64,256]{1,0:T(8,128)S(1)}, ...), condition=%wide.region_9.9_spmd.clone.clone, body=%wide.region_7.8_spmd.clone.clone.sunk | while | flops 50496128 | bytes 1198381 | solution.py:78
  437.6 33.7 %while.186 = (s32[]{:T(128)}, f32[64,256]{1,0:T(8,128)S(1)}, f32[2,128,64]{1,2,0:T(8,128)}, f32[2,128]{1,0:T(2,128)}, f32[2,128,128]{2,1,0:T(8,128)}, /*index=5*...) while((s32[]{:T(128)}, f32[64,256]{1,0:T(8,128)S(1)}, ...), condition=%wide.region_19.19_spmd.clone.clone, body=%wide.region_10.18_spmd.clone.clone.sunk | while | flops 126174464 | bytes 2319733 | solution.py:78
  482.2 3.0 constant_dynamic-slice_fusion.26
  489.1 12.2 %while.185 = (s32[]{:T(128)}, f32[64,256]{1,0:T(8,128)S(1)}, f32[2,128,128]{2,1,0:T(8,128)S(1)}, f32[2,128,128]{2,1,0:T(8,128)S(1)}, f32[2,1,128]{2,1,0:T(1,128)...) while((s32[]{:T(128)}, f32[64,256]{1,0:T(8,128)S(1)}, ...), condition=%wide.region_9.9_spmd.clone.clone, body=%wide.region_7.8_spmd.clone.clone.sunk | while | flops 50496128 | bytes 1198381 | solution.py:78
  505.5 33.7 %while.186 = (s32[]{:T(128)}, f32[64,256]{1,0:T(8,128)S(1)}, f32[2,128,64]{1,2,0:T(8,128)}, f32[2,128]{1,0:T(2,128)}, f32[2,128,128]{2,1,0:T(8,128)}, /*index=5*...) while((s32[]{:T(128)}, f32[64,256]{1,0:T(8,128)S(1)}, ...), condition=%wide.region_19.19_spmd.clone.clone, body=%wide.region_10.18_spmd.clone.clone.sunk | while | flops 126174464 | bytes 2319733 | solution.py:78
  550.0 3.0 constant_dynamic-slice_fusion.26
  557.0 12.2 %while.185 = (s32[]{:T(128)}, f32[64,256]{1,0:T(8,128)S(1)}, f32[2,128,128]{2,1,0:T(8,128)S(1)}, f32[2,128,128]{2,1,0:T(8,128)S(1)}, f32[2,1,128]{2,1,0:T(1,128)...) while((s32[]{:T(128)}, f32[64,256]{1,0:T(8,128)S(1)}, ...), condition=%wide.region_9.9_spmd.clone.clone, body=%wide.region_7.8_spmd.clone.clone.sunk | while | flops 50496128 | bytes 1198381 | solution.py:78
  573.4 33.7 %while.186 = (s32[]{:T(128)}, f32[64,256]{1,0:T(8,128)S(1)}, f32[2,128,64]{1,2,0:T(8,128)}, f32[2,128]{1,0:T(2,128)}, f32[2,128,128]{2,1,0:T(8,128)}, /*index=5*...) while((s32[]{:T(128)}, f32[64,256]{1,0:T(8,128)S(1)}, ...), condition=%wide.region_19.19_spmd.clone.clone, body=%wide.region_10.18_spmd.clone.clone.sunk | while | flops 126174464 | bytes 2319733 | solution.py:78
  617.9 3.0 constant_dynamic-slice_fusion.26
  624.8 12.2 %while.185 = (s32[]{:T(128)}, f32[64,256]{1,0:T(8,128)S(1)}, f32[2,128,128]{2,1,0:T(8,128)S(1)}, f32[2,128,128]{2,1,0:T(8,128)S(1)}, f32[2,1,128]{2,1,0:T(1,128)...) while((s32[]{:T(128)}, f32[64,256]{1,0:T(8,128)S(1)}, ...), condition=%wide.region_9.9_spmd.clone.clone, body=%wide.region_7.8_spmd.clone.clone.sunk | while | flops 50496128 | bytes 1198381 | solution.py:78
  641.2 33.7 %while.186 = (s32[]{:T(128)}, f32[64,256]{1,0:T(8,128)S(1)}, f32[2,128,64]{1,2,0:T(8,128)}, f32[2,128]{1,0:T(2,128)}, f32[2,128,128]{2,1,0:T(8,128)}, /*index=5*...) while((s32[]{:T(128)}, f32[64,256]{1,0:T(8,128)S(1)}, ...), condition=%wide.region_19.19_spmd.clone.clone, body=%wide.region_10.18_spmd.clone.clone.sunk | while | flops 126174464 | bytes 2319733 | solution.py:78
  685.7 3.0 constant_dynamic-slice_fusion.26
  692.7 12.2 %while.185 = (s32[]{:T(128)}, f32[64,256]{1,0:T(8,128)S(1)}, f32[2,128,128]{2,1,0:T(8,128)S(1)}, f32[2,128,128]{2,1,0:T(8,128)S(1)}, f32[2,1,128]{2,1,0:T(1,128)...) while((s32[]{:T(128)}, f32[64,256]{1,0:T(8,128)S(1)}, ...), condition=%wide.region_9.9_spmd.clone.clone, body=%wide.region_7.8_spmd.clone.clone.sunk | while | flops 50496128 | bytes 1198381 | solution.py:78
  709.1 33.7 %while.186 = (s32[]{:T(128)}, f32[64,256]{1,0:T(8,128)S(1)}, f32[2,128,64]{1,2,0:T(8,128)}, f32[2,128]{1,0:T(2,128)}, f32[2,128,128]{2,1,0:T(8,128)}, /*index=5*...) while((s32[]{:T(128)}, f32[64,256]{1,0:T(8,128)S(1)}, ...), condition=%wide.region_19.19_spmd.clone.clone, body=%wide.region_10.18_spmd.clone.clone.sunk | while | flops 126174464 | bytes 2319733 | solution.py:78
  753.6 3.0 constant_dynamic-slice_fusion.26
  760.6 12.2 %while.185 = (s32[]{:T(128)}, f32[64,256]{1,0:T(8,128)S(1)}, f32[2,128,128]{2,1,0:T(8,128)S(1)}, f32[2,128,128]{2,1,0:T(8,128)S(1)}, f32[2,1,128]{2,1,0:T(1,128)...) while((s32[]{:T(128)}, f32[64,256]{1,0:T(8,128)S(1)}, ...), condition=%wide.region_9.9_spmd.clone.clone, body=%wide.region_7.8_spmd.clone.clone.sunk | while | flops 50496128 | bytes 1198381 | solution.py:78
  777.0 33.7 %while.186 = (s32[]{:T(128)}, f32[64,256]{1,0:T(8,128)S(1)}, f32[2,128,64]{1,2,0:T(8,128)}, f32[2,128]{1,0:T(2,128)}, f32[2,128,128]{2,1,0:T(8,128)}, /*index=5*...) while((s32[]{:T(128)}, f32[64,256]{1,0:T(8,128)S(1)}, ...), condition=%wide.region_19.19_spmd.clone.clone, body=%wide.region_10.18_spmd.clone.clone.sunk | while | flops 126174464 | bytes 2319733 | solution.py:78
  823.5 9.3 %all-to-all-start.7 = ((f32[32,8,8]{1,2,0:T(8,128)}), f32[32,8,8]{1,2,0:T(8,128)S(1)}, u32[]{:S(2)}, u32[]{:S(2)}) async-start(f32[32,8,8]{1,2,0:T(8,128)} %copy.135), calls=%async_computation.7 | async-start | bytes 262144 | tf_op jit(solution)/shard_map/all_to_all | solution.py:192
  834.4 7.5 all-to-all-done.7
  841.9 4.4 all-to-all-start.6
  849.3 6.7 all-to-all-done.6
  856.0 6.3 all-to-all-start.5
  863.3 3.8 collective-permute-start.1
  868.4 2.9 collective-permute-done.1
  873.0 8.9 all-to-all-start.4
  883.9 9.4 %all-to-all-done.4 = bf16[32,8,512]{2,1,0:T(8,128)(2,1)S(1)} async-done(((bf16[32,8,512]{2,1,0:T(8,128)(2,1)}), bf16[32,8,512]{2,1,0:T(8,128)(2,1)S(1)}, u32[]{:S(2)}, u32[]{:S(2)}) %all-to-all-start.4) | async-done | bytes 262176 | tf_op jit(solution)/shard_map/all_to_all | solution.py:188
  (1221 shorter events, 564.0 us)
Async XLA Ops:
  7.2 73.2 %copy-start.11 = (f32[4,512]{1,0:T(4,128)S(1)}, f32[4,512]{1,0:T(4,128)}, u32[]{:S(2)}) copy-start(f32[4,512]{1,0:T(4,128)} %param.26) | copy-start | bytes 24580
  7.2 92.8 %copy-start.12 = (f32[512]{0:T(512)S(1)}, f32[512]{0:T(512)}, u32[]{:S(2)}) copy-start(f32[512]{0:T(512)} %param.27) | copy-start | bytes 6148
  42.6 27.8 %all-to-all-start.2 = ((bf16[32,8,2048]{2,1,0:T(8,128)(2,1)}), bf16[32,8,2048]{2,1,0:T(8,128)(2,1)S(1)}, u32[]{:S(2)}, u32[]{:S(2)}) async-start(bf16[32,8,2048]{2,1,0:T(8,128)(2,1)} %stack.2), calls=%async_computation.2 | async-start | bytes 2097152 | tf_op jit(solution)/shard_map/all_to_all | solution.py:104
  47.7 88.0 %all-gather.7.cloned.1.call-start = ((), (), s32[]{:S(2)}) async-start(), calls=%async_computation.8 | async-start | bytes 1081344 | tf_op jit(solution)/shard_map/all_gather | solution.py:102
  48.4 151.5 %all-gather.9.cloned.1.call-start = ((), (), s32[]{:S(2)}) async-start(), calls=%async_computation.9 | async-start | bytes 8912896 | tf_op jit(solution)/shard_map/all_gather | solution.py:22
  70.5 129.5 %copy-start.2 = (bf16[256,256]{1,0:T(8,128)(2,1)}, bf16[256,256]{1,0:T(8,128)(2,1)S(1)}, u32[]{:S(2)}) copy-start(bf16[256,256]{1,0:T(8,128)(2,1)S(1)} %get-tuple-element.2368) | copy-start | bytes 393220
  72.3 17.6 %all-to-all-start.3 = ((bf16[8,32,512]{2,0,1:T(8,128)(2,1)}), bf16[8,32,512]{2,0,1:T(8,128)(2,1)S(1)}, u32[]{:S(2)}, u32[]{:S(2)}) async-start(bf16[8,32,512]{2,0,1:T(8,128)(2,1)} %bitcast.523), calls=%async_computation.3 | async-start | bytes 524288 | tf_op jit(solution)/shard_map/all_to_all | solution.py:97
  80.3 179.2 %all-gather.11.cloned.1.call-start = ((), (), s32[]{:S(2)}) async-start(), calls=%async_computation.10 | async-start | bytes 8912896 | tf_op jit(solution)/shard_map/all_gather | solution.py:22
  89.9 9.9 %collective-permute-start = (bf16[3,512]{1,0:T(4,128)(2,1)S(1)}, bf16[3,512]{1,0:T(4,128)(2,1)S(1)}, u32[]{:S(2)}, u32[]{:S(2)}) collective-permute-start(bf16[3,512]{1,0:T(4,128)(2,1)S(1)} %slice.212), channel_id=1, source_target_pairs={{0,32},{32,64},{64,96},{96,128},{128,160},{160,192},{192,224},{224... | collective-permute-start | bytes 9224 | tf_op jit(solution)/shard_map/ppermute | solution.py:17
  136.6 122.9 %copy-start.1 = (bf16[256,256]{1,0:T(8,128)(2,1)}, bf16[256,256]{1,0:T(8,128)(2,1)S(1)}, u32[]{:S(2)}) copy-start(bf16[256,256]{1,0:T(8,128)(2,1)S(1)} %get-tuple-element.2370) | copy-start | bytes 393220
  279.6 6.3 copy-start.3
  279.6 6.3 copy-start.4
  279.6 6.3 copy-start.5
  279.6 6.3 copy-start.9
  298.9 2.2 copy-start.13
  346.4 6.3 copy-start.3
  346.4 6.3 copy-start.4
  346.4 6.3 copy-start.5
  346.4 6.3 copy-start.9
  414.3 6.3 copy-start.3
  414.3 6.3 copy-start.4
  414.3 6.3 copy-start.5
  414.3 6.3 copy-start.9
  482.1 6.3 copy-start.3
  482.1 6.3 copy-start.4
  482.1 6.3 copy-start.5
  482.1 6.3 copy-start.9
  550.0 6.3 copy-start.3
  550.0 6.3 copy-start.4
  550.0 6.3 copy-start.5
  550.0 6.3 copy-start.9
  617.8 6.3 copy-start.3
  617.8 6.3 copy-start.4
  617.9 6.3 copy-start.5
  617.9 6.3 copy-start.9
  685.7 6.3 copy-start.3
  685.7 6.3 copy-start.4
  685.7 6.3 copy-start.5
  685.7 6.3 copy-start.9
  753.6 6.3 copy-start.3
  753.6 6.3 copy-start.4
  753.6 6.3 copy-start.5
  753.6 6.3 copy-start.9
  823.5 18.4 %all-to-all-start.7 = ((f32[32,8,8]{1,2,0:T(8,128)}), f32[32,8,8]{1,2,0:T(8,128)S(1)}, u32[]{:S(2)}, u32[]{:S(2)}) async-start(f32[32,8,8]{1,2,0:T(8,128)} %copy.135), calls=%async_computation.7 | async-start | bytes 262144 | tf_op jit(solution)/shard_map/all_to_all | solution.py:192
  841.9 14.1 %all-to-all-start.6 = ((f32[32,8,256]{2,1,0:T(8,128)}), f32[32,8,256]{2,1,0:T(8,128)S(1)}, u32[]{:S(2)}, u32[]{:S(2)}) async-start(f32[32,8,256]{2,1,0:T(8,128)} %bitcast.45), calls=%async_computation.6 | async-start | bytes 524288 | tf_op jit(solution)/shard_map/all_to_all | solution.py:194
  856.0 17.0 %all-to-all-start.5 = ((f32[32,8,256]{2,1,0:T(8,128)}), f32[32,8,256]{2,1,0:T(8,128)S(1)}, u32[]{:S(2)}, u32[]{:S(2)}) async-start(f32[32,8,256]{2,1,0:T(8,128)} %bitcast.40), calls=%async_computation.5 | async-start | bytes 524288 | tf_op jit(solution)/shard_map/all_to_all | solution.py:193
  863.3 8.0 collective-permute-start.1
  873.0 20.3 %all-to-all-start.4 = ((bf16[32,8,512]{2,1,0:T(8,128)(2,1)}), bf16[32,8,512]{2,1,0:T(8,128)(2,1)S(1)}, u32[]{:S(2)}, u32[]{:S(2)}) async-start(bf16[32,8,512]{2,1,0:T(8,128)(2,1)} %bitcast.36), calls=%async_computation.4 | async-start | bytes 524288 | tf_op jit(solution)/shard_map/all_to_all | solution.py:188
  (47 other events, 104.3 us)
Sparse Core Ops, SparseCore 0:
  51.7 83.8 all-gather.6
  137.7 62.1 all-gather.8
  202.1 57.3 all-gather.10
